TPU v7x, 32 devices: a whole 2x2x4 slice. The times are simulated.
32 devices in a mesh: groups: 2 (over y), ep: 8 (over z, x), tp: 2 (over core).
Axes of the slice: x: 2, y: 2, z: 4, core: 2. Of those that a mesh axis runs over, the one named last changes fastest.
Arguments:
- hidden: bfloat16 [128, 4096], P(('groups', 'ep', 'tp')), parts along dimension 0, may hold values from -6 to 6
- norm_gain: float32 [4096], replicated, may hold values from 0.5 to 1.5
- rot_left: float32 [64, 64], replicated, may hold values from -0.75 to 0.75
- rot_right: float32 [64, 64], replicated, may hold values from -0.75 to 0.75
- expert_ids: int32 [128, 8], P(('groups', 'ep')), parts along dimension 0, may hold values from 0 to 63, as said below
- gate_weights: float32 [128, 8], P(('groups', 'ep')), parts along dimension 0, may hold values from 0.05 to 1
- w_gate: bfloat16 [128, 4096, 384], P('ep', 'tp'), may hold values from -0.09375 to 0.09375
- w_up: bfloat16 [128, 4096, 384], P('ep', 'tp'), may hold values from -0.09375 to 0.09375
- w_down: bfloat16 [128, 384, 4096], P('ep', None, 'tp'), may hold values from -0.21875 to 0.21875
- unit_scales: float32 [128, 2, 384], P('ep'), may hold values from 0.25 to 1.75
Outputs:
- moe_out: bfloat16 [128, 4096], P(('groups', 'ep', 'tp')), parts along dimension 0
There are 2 independent parts, one for each index of `groups`. A program takes and returns all parts, laid end to end along the dimension named above; an argument that names none is the same for every part. Nothing has to cross between parts.
Inputs may be any that keep to these rules, and one draw needn't show every extreme that they name: `expert_ids`: each row names 8 different experts. In each aligned block of 8 rows (the rows of one index of ep) no expert is named by more than 2 rows, and in every block some experts are named by exactly 2 rows; every expert is named by exactly 2 rows in some block.
All inputs are finite; a program needn't handle non-finite values.
Results may differ from a plain program's by a relative error of at most 0.0082.
Values may be sent and summed in bfloat16 or wider, within the bound.
A program may use at most 128 MiB of HBM per device.

v0:
```python
import jax
import jax.numpy as jnp
from jax import lax
from jax.sharding import PartitionSpec as P

EXPERTS = 64


def rotate(hidden, norm_gain, rot_left, rot_right):
    values = hidden.astype(jnp.float32)
    mean_square = jnp.mean(values * values, axis=1, keepdims=True)
    normed = values * lax.rsqrt(mean_square + 1e-06) * norm_gain[None, :]
    factor = rot_left.shape[0]
    square = normed.reshape(-1, factor, factor)
    turned = jnp.einsum("ij,rjk->rik", rot_left, square, precision=lax.Precision.HIGHEST)
    turned = jnp.einsum("rik,lk->ril", turned, rot_right, precision=lax.Precision.HIGHEST)
    return turned.reshape(normed.shape).astype(jnp.bfloat16)


def activate(gate_sum, up_sum, unit_scales):
    gate_scale = unit_scales[None, :, 0, None, :]
    up_scale = unit_scales[None, :, 1, None, :]
    return (jax.nn.silu(gate_sum * gate_scale) * (up_sum * up_scale)).astype(jnp.bfloat16)


def body(
    hidden,
    norm_gain,
    rot_left,
    rot_right,
    expert_ids,
    gate_weights,
    w_gate,
    w_up,
    w_down,
    unit_scales,
):
    ep_count = lax.axis_size("ep")
    group_rows = expert_ids.shape[0]
    top_count = expert_ids.shape[1]
    held_halves = w_gate.shape[0]
    capacity = 5 * group_rows * top_count // (2 * EXPERTS)
    rotated = rotate(hidden, norm_gain, rot_left, rot_right)
    pair_rows = lax.all_to_all(rotated, "tp", split_axis=1, concat_axis=0, tiled=True)
    weight_norm = (gate_weights / jnp.sum(gate_weights, axis=1, keepdims=True)).astype(jnp.bfloat16)
    onehot = (
        expert_ids.reshape(-1)[:, None] == jnp.arange(EXPERTS, dtype=jnp.int32)[None, :]
    ).astype(jnp.int32)
    slot_rank = jnp.sum((jnp.cumsum(onehot, axis=0) - onehot) * onehot, axis=1).reshape(
        group_rows, top_count
    )
    low_target = expert_ids * capacity + slot_rank
    targets = (low_target, low_target + EXPERTS * capacity)
    line_count = 2 * EXPERTS * capacity
    line_index = jnp.arange(line_count, dtype=jnp.int32)[:, None, None]
    matches = jnp.zeros((line_count, group_rows, top_count), jnp.float32)
    for target in targets:
        matches = matches + (line_index == target[None, :, :]).astype(jnp.float32)
    dispatch = jnp.sum(matches, axis=2).astype(jnp.bfloat16)
    outgoing = jnp.dot(dispatch, pair_rows, preferred_element_type=jnp.float32).astype(jnp.bfloat16)
    outgoing = outgoing.reshape(ep_count, held_halves * capacity, -1)
    received = lax.all_to_all(outgoing, "ep", split_axis=0, concat_axis=0, tiled=True)
    received = received.reshape(ep_count, held_halves, capacity, -1)
    gate_sum = jnp.einsum("shcd,hdf->shcf", received, w_gate, preferred_element_type=jnp.float32)
    up_sum = jnp.einsum("shcd,hdf->shcf", received, w_up, preferred_element_type=jnp.float32)
    gate_sum, up_sum = (
        lax.psum_scatter(gate_sum, "tp", scatter_dimension=0, tiled=True),
        lax.psum_scatter(up_sum, "tp", scatter_dimension=0, tiled=True),
    )
    half_hidden = activate(gate_sum, up_sum, unit_scales)
    hidden_units = lax.all_gather(half_hidden, "tp", axis=0, tiled=True)
    partial_value = jnp.einsum(
        "shcf,hfd->shcd", hidden_units, w_down, preferred_element_type=jnp.float32
    ).astype(jnp.bfloat16)
    flat_partial = partial_value.reshape(ep_count, held_halves * capacity, -1)
    returned = lax.all_to_all(flat_partial, "ep", split_axis=0, concat_axis=0, tiled=True)
    returned = returned.reshape(2 * EXPERTS * capacity, -1)
    expert_out = (
        returned[: EXPERTS * capacity].astype(jnp.float32)
        + returned[EXPERTS * capacity :].astype(jnp.float32)
    ).astype(jnp.bfloat16)
    line_spot = (expert_ids * capacity + slot_rank)[:, :, None]
    out_lines = EXPERTS * capacity
    columns = jnp.arange(out_lines, dtype=jnp.int32)[None, None, :]
    hits = (columns == line_spot).astype(jnp.float32)
    mixing = jnp.sum(weight_norm.astype(jnp.float32)[:, :, None] * hits, axis=1).astype(
        jnp.bfloat16
    )
    combined = jnp.dot(mixing, expert_out, preferred_element_type=jnp.float32).astype(jnp.bfloat16)
    return lax.all_to_all(combined, "tp", split_axis=0, concat_axis=1, tiled=True)


def solution(mesh):
    placed = (
        P(("groups", "ep", "tp"), None),
        P(),
        P(),
        P(),
        P(("groups", "ep"), None),
        P(("groups", "ep"), None),
        P("ep", "tp", None),
        P("ep", "tp", None),
        P("ep", None, "tp"),
        P("ep", None, None),
    )
    return jax.shard_map(
        body, mesh=mesh, in_specs=placed, out_specs=P(("groups", "ep", "tp"), None), check_vma=False
    )
```

profile of v0, /device:TPU:0, one launch (start us, length us, event | category | flops | bytes accessed | tf_op | source)
XLA Modules:
  0.0 139.3 jit_solution(9439551862724553802)
XLA Ops:
  6.5 0.9 fusion.16
  7.5 0.8 fusion.17
  8.4 0.4 convolution_bitcast_fusion
  8.8 1.1 convolution_convert_fusion.2
  10.1 0.6 copy.32
  10.7 3.3 %all-to-all-start = ((bf16[4,2,2048]{2,0,1:T(4,128)(2,1)}), bf16[4,2,2048]{2,0,1:T(4,128)(2,1)S(1)}, u32[]{:S(2)}, u32[]{:S(2)}) async-start(bf16[4,2,2048]{2,0,1:T(4,128)(2,1)} %copy.32), calls=%async_computation | async-start | bytes 65536 | tf_op jit(solution)/shard_map/all_to_all | solution.py:44
  14.1 0.8 eq.27
  15.3 0.7 broadcast_add_fusion
  16.1 0.5 convolution_convert_fusion
  16.6 33.4 %all_to_all.45 = bf16[8,32,2048]{2,1,0:T(8,128)(2,1)S(1)} all-to-all(bf16[8,32,2048]{2,1,0:T(8,128)(2,1)S(1)} %bitcast.58), channel_id=1, replica_groups=mesh['groups'=2,'ep'=8,'tp'=2] {'ep'}, dimensions={0} | all-to-all | bytes 2097152 | tf_op jit(solution)/shard_map/all_to_all | solution.py:62
  50.0 0.6 copy.33
  50.6 9.9 %fusion.9 = f32[8,16,2,384]{3,0,2,1:T(8,128)S(1)} fusion(bf16[8,16,2,2048]{3,0,2,1:T(8,128)(2,1)S(1)} %bitcast.55, bf16[16,2048,384]{2,1,0:T(8,128)(2,1)} %param.16), kind=kOutput, calls=%fused_computation.9 | convolution fusion | flops 402653184 | bytes 26607616 | tf_op jit(solution)/shard_map/shcd,hdf->shcf/dot_general | solution.py:64
  60.5 0.9 copy.34
  61.4 10.1 %fusion.12 = f32[8,16,2,384]{3,0,2,1:T(8,128)S(1)} fusion(bf16[8,16,2,2048]{3,0,2,1:T(8,128)(2,1)S(1)} %bitcast.56, bf16[16,2048,384]{2,1,0:T(8,128)(2,1)} %param.17), kind=kOutput, calls=%fused_computation.10 | convolution fusion | flops 402653184 | bytes 26607616 | tf_op jit(solution)/shard_map/shcd,hdf->shcf/dot_general | solution.py:65
  71.6 0.9 copy.36
  72.6 7.1 %reduce-scatter.5.cloned.1.call-done = f32[4,16,2,384]{3,1,2,0:T(8,128)} async-done(((f32[8,16,2,384]{3,1,2,0:T(8,128)}), f32[4,16,2,384]{3,1,2,0:T(8,128)}) %reduce-scatter.5.cloned.1.call-update) | async-done | bytes 196624 | tf_op jit(solution)/shard_map/reduce_scatter | solution.py:68
  79.6 1.1 multiply_convert_fusion
  80.7 1.9 %all_gather.3 = bf16[8,16,2,384]{3,1,2,0:T(8,128)(2,1)S(1)} all-gather(bf16[4,16,2,384]{3,1,2,0:T(8,128)(2,1)S(1)} %multiply_convert_fusion), channel_id=1, replica_groups=mesh['groups'=2,'ep'=8,'tp'=2] {'tp'}, dimensions={0}, use_global_device_ids=true | all-gather | bytes 294912 | tf_op jit(solution)/shard_map/all_gather | solution.py:71
  82.7 11.5 %fusion.6 = bf16[16,8,2,2048]{3,1,2,0:T(8,128)(2,1)S(1)} fusion(bf16[16,384,2048]{2,1,0:T(8,128)(2,1)} %param.18, bf16[8,16,2,384]{3,1,2,0:T(8,128)(2,1)S(1)} %all_gather.3), kind=kOutput, calls=%fused_computation.6 | convolution fusion | flops 403177472 | bytes 26411008 | tf_op jit(solution)/shard_map/shcf,hfd->shcd/dot_general | solution.py:72
  94.2 1.6 %copy.39 = bf16[8,32,2048]{2,1,0:T(8,128)(2,1)} copy(bf16[8,32,2048]{2,0,1:T(8,128)(2,1)S(1)} %bitcast.57) | data formatting | bytes 2097152 | tf_op jit(solution)/shard_map/reshape | solution.py:75
  95.8 5.7 %all-to-all-start.2 = ((bf16[8,32,2048]{2,1,0:T(8,128)(2,1)}), bf16[8,32,2048]{2,1,0:T(8,128)(2,1)S(1)}, u32[]{:S(2)}, u32[]{:S(2)}) async-start(bf16[8,32,2048]{2,1,0:T(8,128)(2,1)} %copy.39), calls=%async_computation.4 | async-start | bytes 2097152 | tf_op jit(solution)/shard_map/all_to_all | solution.py:76
  101.8 26.0 %all-to-all-done.2 = bf16[8,32,2048]{2,1,0:T(8,128)(2,1)S(1)} async-done(((bf16[8,32,2048]{2,1,0:T(8,128)(2,1)}), bf16[8,32,2048]{2,1,0:T(8,128)(2,1)S(1)}, u32[]{:S(2)}, u32[]{:S(2)}) %all-to-all-start.2) | async-done | bytes 1048608 | tf_op jit(solution)/shard_map/all_to_all | solution.py:76
  128.1 3.7 %all_to_all.46 = bf16[2,4,2048]{2,1,0:T(4,128)(2,1)S(1)} all-to-all(bf16[2,4,2048]{2,1,0:T(4,128)(2,1)S(1)} %all_to_all.37), channel_id=1, replica_groups=mesh['groups'=2,'ep'=8,'tp'=2] {'tp'}, dimensions={0} | all-to-all | bytes 65536 | tf_op jit(solution)/shard_map/all_to_all | solution.py:90
  131.9 0.6 copy.53
  (31 shorter events, 1.6 us)
Async XLA Ops:
  6.5 1.9 %copy-start = (f32[64,64]{1,0:T(8,128)S(1)}, f32[64,64]{1,0:T(8,128)}, u32[]{:S(2)}) copy-start(f32[64,64]{1,0:T(8,128)} %param.12) | copy-start | bytes 49156
  10.7 5.2 %all-to-all-start = ((bf16[4,2,2048]{2,0,1:T(4,128)(2,1)}), bf16[4,2,2048]{2,0,1:T(4,128)(2,1)S(1)}, u32[]{:S(2)}, u32[]{:S(2)}) async-start(bf16[4,2,2048]{2,0,1:T(4,128)(2,1)} %copy.32), calls=%async_computation | async-start | bytes 65536 | tf_op jit(solution)/shard_map/all_to_all | solution.py:44
  14.0 58.5 %reduce-scatter.3.cloned.1.call-start = ((), (), s32[]{:S(2)}) async-start(), calls=%async_computation.6 | async-start | bytes 589824 | tf_op jit(solution)/shard_map/reduce_scatter | solution.py:67
  50.6 21.9 %copy-start.2 = (f32[16,2,384]{2,1,0:T(2,128)S(1)}, f32[16,2,384]{2,1,0:T(2,128)}, u32[]{:S(2)}) copy-start(f32[16,2,384]{2,1,0:T(2,128)} %param.19) | copy-start | bytes 147460
  61.4 18.3 %reduce-scatter.5.cloned.1.call-start = ((), (), s32[]{:S(2)}) async-start(), calls=%async_computation.7 | async-start | bytes 589824 | tf_op jit(solution)/shard_map/reduce_scatter | solution.py:68
  61.4 71.1 %copy-start.1 = (f32[64,64]{1,0:T(8,128)S(1)}, f32[64,64]{1,0:T(8,128)}, u32[]{:S(2)}) copy-start(f32[64,64]{1,0:T(8,128)} %param.12) | copy-start | bytes 49156
  71.6 30.0 %copy-start.3 = (f32[8,8]{1,0:T(8,128)S(1)}, f32[8,8]{1,0:T(8,128)}, u32[]{:S(2)}) copy-start(f32[8,8]{1,0:T(8,128)} %param.15) | copy-start | bytes 772
  95.8 32.0 %all-to-all-start.2 = ((bf16[8,32,2048]{2,1,0:T(8,128)(2,1)}), bf16[8,32,2048]{2,1,0:T(8,128)(2,1)S(1)}, u32[]{:S(2)}, u32[]{:S(2)}) async-start(bf16[8,32,2048]{2,1,0:T(8,128)(2,1)} %copy.39), calls=%async_computation.4 | async-start | bytes 2097152 | tf_op jit(solution)/shard_map/all_to_all | solution.py:76
Sparse Core Ops, SparseCore 0:
  61.5 6.8 reduce-scatter.2
  72.6 7.0 reduce-scatter.4
where the time goes:
time: 140 us; the launch traced here: 139 us
  blocking collectives  39.1 us (28%)
  matrix products  33.7 us (24%)
  waiting for transfers between devices  33.1 us (24%)
  between operations  13.6 us (10%)
  starting transfers between devices  9.08 us (6%)
  local copies, waits for them, and re-layouts  6.33 us (5%)
  other arithmetic  4.44 us (3%)
    all_to_all x1, blocking collectives, body(): lax.all_to_all(outgoing, 'ep', split_axis=0, concat_axis=0, tiled=True)  33.4 us
    all_to_all x1, waiting for transfers between devices, body(): lax.all_to_all(flat_partial, 'ep', split_axis=0, concat_axis=0, tiled=True)  26 us
    dot_general x1, matrix products, body(): jnp.einsum('shcf,hfd->shcd', hidden_units, w_down, preferred_element_type...  11.5 us
    dot_general x1, matrix products, body(): jnp.einsum('shcd,hdf->shcf', received, w_up, preferred_element_type=jnp.f...  10.1 us
    dot_general x1, matrix products, body(): jnp.einsum('shcd,hdf->shcf', received, w_gate, preferred_element_type=jnp...  9.91 us
    reduce_scatter x1, waiting for transfers between devices, body(): lax.psum_scatter(up_sum, 'tp', scatter_dimension=0, tiled=True)  7.08 us
    all_to_all x1, starting transfers between devices, body(): lax.all_to_all(flat_partial, 'ep', split_axis=0, concat_axis=0, tiled=True)  5.74 us
    all_to_all x1, blocking collectives, body(): lax.all_to_all(combined, 'tp', split_axis=0, concat_axis=1, tiled=True)  3.75 us
  transfers between devices with their start and end apart: 4, of which 2 were waited for; matrix products, arithmetic and copies ran while one was open for 9% of the time, Pallas kernels for 0%

commit v1 on v0

--- a/solution.py
+++ b/solution.py
@@ -87,7 +87,20 @@
         jnp.bfloat16
     )
     combined = jnp.dot(mixing, expert_out, preferred_element_type=jnp.float32).astype(jnp.bfloat16)
-    return lax.all_to_all(combined, "tp", split_axis=0, concat_axis=1, tiled=True)
+
+    def _part_islands(page, group_axis):
+        heard = jnp.concatenate(
+            lax.all_to_all(
+                jnp.stack(jnp.split(page, lax.axis_size(group_axis), axis=0), axis=0),
+                group_axis,
+                0,
+                0,
+            ),
+            axis=1,
+        )
+        return heard
+
+    return _part_islands(combined, "tp")
 
 
 def solution(mesh):

time: 140 us -> 140 us (level)
  no operation moved by 1% of the time
where the time goes in v1:
time: 140 us; the launch traced here: 139 us
  blocking collectives  39.1 us (28%)
  matrix products  33.7 us (24%)
  waiting for transfers between devices  33.1 us (24%)
  between operations  13.6 us (10%)
  starting transfers between devices  9.08 us (6%)
  local copies, waits for them, and re-layouts  6.33 us (5%)
  other arithmetic  4.46 us (3%)
    all_to_all x1, blocking collectives, body(): lax.all_to_all(outgoing, 'ep', split_axis=0, concat_axis=0, tiled=True)  33.4 us
    all_to_all x1, waiting for transfers between devices, body(): lax.all_to_all(flat_partial, 'ep', split_axis=0, concat_axis=0, tiled=True)  26 us
    dot_general x1, matrix products, body(): jnp.einsum('shcf,hfd->shcd', hidden_units, w_down, preferred_element_type...  11.5 us
    dot_general x1, matrix products, body(): jnp.einsum('shcd,hdf->shcf', received, w_up, preferred_element_type=jnp.f...  10.1 us
    dot_general x1, matrix products, body(): jnp.einsum('shcd,hdf->shcf', received, w_gate, preferred_element_type=jnp...  9.91 us
    reduce_scatter x1, waiting for transfers between devices, body(): lax.psum_scatter(up_sum, 'tp', scatter_dimension=0, tiled=True)  7.08 us
    all_to_all x1, starting transfers between devices, body(): lax.all_to_all(flat_partial, 'ep', split_axis=0, concat_axis=0, tiled=True)  5.74 us
    all_to_all x1, blocking collectives, _part_islands(): lax.all_to_all(jnp.stack(jnp.split(page, lax.axis_size(group_axis), axis=...  3.75 us
  transfers between devices with their start and end apart: 4, of which 2 were waited for; matrix products, arithmetic and copies ran while one was open for 9% of the time, Pallas kernels for 0%

profile of v1, /device:TPU:0, one launch (start us, length us, event | category | flops | bytes accessed | tf_op | source)
XLA Modules:
  0.0 139.3 jit_solution(17063286577456706128)
XLA Ops:
  6.5 0.9 fusion.16
  7.5 0.8 fusion.17
  8.4 0.4 convolution_bitcast_fusion
  8.8 1.1 convolution_convert_fusion.2
  10.1 0.6 copy.29
  10.7 3.3 %all-to-all-start = ((bf16[4,2,2048]{2,0,1:T(4,128)(2,1)}), bf16[4,2,2048]{2,0,1:T(4,128)(2,1)S(1)}, u32[]{:S(2)}, u32[]{:S(2)}) async-start(bf16[4,2,2048]{2,0,1:T(4,128)(2,1)} %copy.29), calls=%async_computation | async-start | bytes 65536 | tf_op jit(solution)/shard_map/all_to_all | solution.py:44
  14.1 0.8 eq.27
  15.3 0.7 broadcast_add_fusion
  16.1 0.5 convolution_convert_fusion
  16.6 33.4 %all_to_all.31 = bf16[8,32,2048]{2,1,0:T(8,128)(2,1)S(1)} all-to-all(bf16[8,32,2048]{2,1,0:T(8,128)(2,1)S(1)} %bitcast.62), channel_id=1, replica_groups=mesh['groups'=2,'ep'=8,'tp'=2] {'ep'}, dimensions={0} | all-to-all | bytes 2097152 | tf_op jit(solution)/shard_map/all_to_all | solution.py:62
  50.0 0.6 copy.30
  50.6 9.9 %fusion.9 = f32[8,16,2,384]{3,0,2,1:T(8,128)S(1)} fusion(bf16[8,16,2,2048]{3,0,2,1:T(8,128)(2,1)S(1)} %bitcast.59, bf16[16,2048,384]{2,1,0:T(8,128)(2,1)} %param.16), kind=kOutput, calls=%fused_computation.9 | convolution fusion | flops 402653184 | bytes 26607616 | tf_op jit(solution)/shard_map/shcd,hdf->shcf/dot_general | solution.py:64
  60.5 0.9 copy.31
  61.4 10.1 %fusion.12 = f32[8,16,2,384]{3,0,2,1:T(8,128)S(1)} fusion(bf16[8,16,2,2048]{3,0,2,1:T(8,128)(2,1)S(1)} %bitcast.60, bf16[16,2048,384]{2,1,0:T(8,128)(2,1)} %param.17), kind=kOutput, calls=%fused_computation.10 | convolution fusion | flops 402653184 | bytes 26607616 | tf_op jit(solution)/shard_map/shcd,hdf->shcf/dot_general | solution.py:65
  71.6 0.9 copy.33
  72.6 7.1 %reduce-scatter.5.cloned.1.call-done = f32[4,16,2,384]{3,1,2,0:T(8,128)} async-done(((f32[8,16,2,384]{3,1,2,0:T(8,128)}), f32[4,16,2,384]{3,1,2,0:T(8,128)}) %reduce-scatter.5.cloned.1.call-update) | async-done | bytes 196624 | tf_op jit(solution)/shard_map/reduce_scatter | solution.py:68
  79.6 1.1 multiply_convert_fusion
  80.7 1.9 %all_gather.3 = bf16[8,16,2,384]{3,1,2,0:T(8,128)(2,1)S(1)} all-gather(bf16[4,16,2,384]{3,1,2,0:T(8,128)(2,1)S(1)} %multiply_convert_fusion), channel_id=1, replica_groups=mesh['groups'=2,'ep'=8,'tp'=2] {'tp'}, dimensions={0}, use_global_device_ids=true | all-gather | bytes 294912 | tf_op jit(solution)/shard_map/all_gather | solution.py:71
  82.7 11.5 %fusion.6 = bf16[16,8,2,2048]{3,1,2,0:T(8,128)(2,1)S(1)} fusion(bf16[16,384,2048]{2,1,0:T(8,128)(2,1)} %param.18, bf16[8,16,2,384]{3,1,2,0:T(8,128)(2,1)S(1)} %all_gather.3), kind=kOutput, calls=%fused_computation.6 | convolution fusion | flops 403177472 | bytes 26411008 | tf_op jit(solution)/shard_map/shcf,hfd->shcd/dot_general | solution.py:72
  94.2 1.6 %copy.36 = bf16[8,32,2048]{2,1,0:T(8,128)(2,1)} copy(bf16[8,32,2048]{2,0,1:T(8,128)(2,1)S(1)} %bitcast.61) | data formatting | bytes 2097152 | tf_op jit(solution)/shard_map/reshape | solution.py:75
  95.8 5.7 %all-to-all-start.2 = ((bf16[8,32,2048]{2,1,0:T(8,128)(2,1)}), bf16[8,32,2048]{2,1,0:T(8,128)(2,1)S(1)}, u32[]{:S(2)}, u32[]{:S(2)}) async-start(bf16[8,32,2048]{2,1,0:T(8,128)(2,1)} %copy.36), calls=%async_computation.4 | async-start | bytes 2097152 | tf_op jit(solution)/shard_map/all_to_all | solution.py:76
  101.8 26.0 %all-to-all-done.2 = bf16[8,32,2048]{2,1,0:T(8,128)(2,1)S(1)} async-done(((bf16[8,32,2048]{2,1,0:T(8,128)(2,1)}), bf16[8,32,2048]{2,1,0:T(8,128)(2,1)S(1)}, u32[]{:S(2)}, u32[]{:S(2)}) %all-to-all-start.2) | async-done | bytes 1048608 | tf_op jit(solution)/shard_map/all_to_all | solution.py:76
  128.1 3.7 %all_to_all.32 = bf16[2,4,2048]{2,1,0:T(4,128)(2,1)S(1)} all-to-all(bf16[2,4,2048]{2,1,0:T(4,128)(2,1)S(1)} %pad_maximum_fusion), channel_id=1, replica_groups=mesh['groups'=2,'ep'=8,'tp'=2] {'tp'}, dimensions={0} | all-to-all | bytes 65536 | tf_op jit(solution)/shard_map/all_to_all | solution.py:93
  131.9 0.6 copy.49
  (32 shorter events, 1.7 us)
Async XLA Ops:
  6.5 1.9 %copy-start = (f32[64,64]{1,0:T(8,128)S(1)}, f32[64,64]{1,0:T(8,128)}, u32[]{:S(2)}) copy-start(f32[64,64]{1,0:T(8,128)} %param.12) | copy-start | bytes 49156
  10.7 5.2 %all-to-all-start = ((bf16[4,2,2048]{2,0,1:T(4,128)(2,1)}), bf16[4,2,2048]{2,0,1:T(4,128)(2,1)S(1)}, u32[]{:S(2)}, u32[]{:S(2)}) async-start(bf16[4,2,2048]{2,0,1:T(4,128)(2,1)} %copy.29), calls=%async_computation | async-start | bytes 65536 | tf_op jit(solution)/shard_map/all_to_all | solution.py:44
  14.0 58.5 %reduce-scatter.3.cloned.1.call-start = ((), (), s32[]{:S(2)}) async-start(), calls=%async_computation.6 | async-start | bytes 589824 | tf_op jit(solution)/shard_map/reduce_scatter | solution.py:67
  50.6 21.9 %copy-start.2 = (f32[16,2,384]{2,1,0:T(2,128)S(1)}, f32[16,2,384]{2,1,0:T(2,128)}, u32[]{:S(2)}) copy-start(f32[16,2,384]{2,1,0:T(2,128)} %param.19) | copy-start | bytes 147460
  61.4 18.3 %reduce-scatter.5.cloned.1.call-start = ((), (), s32[]{:S(2)}) async-start(), calls=%async_computation.7 | async-start | bytes 589824 | tf_op jit(solution)/shard_map/reduce_scatter | solution.py:68
  61.4 71.1 %copy-start.1 = (f32[64,64]{1,0:T(8,128)S(1)}, f32[64,64]{1,0:T(8,128)}, u32[]{:S(2)}) copy-start(f32[64,64]{1,0:T(8,128)} %param.12) | copy-start | bytes 49156
  71.6 30.0 %copy-start.3 = (f32[8,8]{1,0:T(8,128)S(1)}, f32[8,8]{1,0:T(8,128)}, u32[]{:S(2)}) copy-start(f32[8,8]{1,0:T(8,128)} %param.15) | copy-start | bytes 772
  95.8 32.0 %all-to-all-start.2 = ((bf16[8,32,2048]{2,1,0:T(8,128)(2,1)}), bf16[8,32,2048]{2,1,0:T(8,128)(2,1)S(1)}, u32[]{:S(2)}, u32[]{:S(2)}) async-start(bf16[8,32,2048]{2,1,0:T(8,128)(2,1)} %copy.36), calls=%async_computation.4 | async-start | bytes 2097152 | tf_op jit(solution)/shard_map/all_to_all | solution.py:76
Sparse Core Ops, SparseCore 0:
  61.5 6.8 reduce-scatter.2
  72.6 7.0 reduce-scatter.4
